TPU v7x, 256 devices: a whole 4x4x8 slice. The times are simulated.
256 devices in a mesh: pb: 64 (over x, y, z_lo), col: 4 (over z_hi, core).
Axes of the slice: x: 4, y: 4, z: 8 (z_hi: 2, z_lo: 4; z = z_hi * 4 + z_lo), core: 2. Of those that a mesh axis runs over, the one named last changes fastest.
Arguments:
- vertex: bfloat16 [3, 256, 448, 896], P(None, 'pb', 'col'), may hold values from -6 to 6
- loop_blocks: bfloat16 [3, 256, 448, 896], P(None, ('pb', 'col')), may hold values from -0.013671875 to 0.013671875
- mixing: float32 [6, 256], replicated, may hold values from -1 to 1
- bond_offsets: int32 [7, 3], replicated, may hold values from -1 to 1
Outputs:
- new_vertex: bfloat16 [3, 256, 448, 896], P(None, 'pb', 'col')
All inputs are finite; a program needn't handle non-finite values.
Results may differ from a plain program's by a relative error of at most 0.007.
Values may be sent and summed in bfloat16 or wider, within the bound.
No kernel may reach another device: no remote copies, remote signals or barrier semaphores. Data moves between devices by JAX's collectives and lax.ppermute only.
A program may use at most 64 MiB of HBM per device.

v0:
```python
import math
import jax
import jax.numpy as jnp
from jax import lax
from jax.sharding import PartitionSpec as P

NB = 7
MX = 8
step_length = 0.25


def mesh_coords(momenta, mesh_y, mesh_z):
    flat_index = jnp.arange(momenta, dtype=jnp.int32)
    coord_x = flat_index // (mesh_y * mesh_z)
    coord_y = flat_index // mesh_z % mesh_y
    coord_z = flat_index % mesh_z
    return (coord_x, coord_y, coord_z)


def phase_tables(momenta, mesh_x, mesh_y, mesh_z):
    coord_x, coord_y, coord_z = mesh_coords(momenta, mesh_y, mesh_z)
    phase_index = (
        coord_x[:, None] * coord_x[None, :] * (mesh_y * mesh_z)
        + coord_y[:, None] * coord_y[None, :] * (mesh_x * mesh_z)
        + coord_z[:, None] * coord_z[None, :] * (mesh_x * mesh_y)
    ) % momenta
    angles = phase_index.astype(jnp.float32) * (2.0 * math.pi / momenta)
    cosine = jnp.cos(angles)
    sine_part = jnp.sin(angles)
    forward = jnp.stack([jnp.stack([cosine, sine_part], 1), jnp.stack([-sine_part, cosine], 1)]) * (
        1.0 / momenta
    )
    backward = jnp.stack([jnp.stack([cosine, -sine_part], 1), jnp.stack([sine_part, cosine], 1)])
    return (forward.astype(jnp.bfloat16), backward.astype(jnp.bfloat16))


def shifted_weights(mixing, bond_offsets, momenta, mesh_x, mesh_y, mesh_z):
    coord_x, coord_y, coord_z = mesh_coords(momenta, mesh_y, mesh_z)
    offsets = bond_offsets[:, None, :] - bond_offsets[None, :, :]
    shift_x = jnp.mod(coord_x[None, None, :] + offsets[:, :, 0:1], mesh_x)
    shift_y = jnp.mod(coord_y[None, None, :] + offsets[:, :, 1:2], mesh_y)
    shift_z = jnp.mod(coord_z[None, None, :] + offsets[:, :, 2:3], mesh_z)
    flat_slot = (shift_x * mesh_y + shift_y) * mesh_z + shift_z
    return jnp.take(mixing, flat_slot, axis=1)


def complex_batch(left_op, right_op):
    half_n = left_op.shape[1]
    real_part = jnp.einsum(
        "bij,bjk->bik", left_op[:, :, :half_n], right_op, preferred_element_type=jnp.float32
    )
    imag_part = jnp.einsum(
        "bij,bjk->bik", left_op[:, :, half_n:], right_op, preferred_element_type=jnp.float32
    )
    return jnp.concatenate(
        [
            real_part[:, :, :half_n] - imag_part[:, :, half_n:],
            real_part[:, :, half_n:] + imag_part[:, :, :half_n],
        ],
        axis=2,
    )


def per_device(vertex, loop_blocks, mixing, bond_offsets):
    groups = lax.axis_size("pb")
    mesh_z = vertex.shape[1]
    row_count = vertex.shape[2]
    full_order = vertex.shape[3] // 2
    narrow = full_order // groups
    momenta = mesh_z * groups
    mesh_y = groups // MX
    forward, backward = phase_tables(momenta, MX, mesh_y, mesh_z)
    weights = shifted_weights(mixing, bond_offsets, momenta, MX, mesh_y, mesh_z)
    split_cols = vertex.reshape(3, mesh_z, row_count, 2, full_order)
    gathered = lax.all_to_all(split_cols, "pb", split_axis=4, concat_axis=1, tiled=True)
    lattice = lax.dot_general(
        gathered, forward, (((3, 1), (0, 1)), ((), ())), preferred_element_type=jnp.float32
    )
    lattice = lax.optimization_barrier(lattice.astype(jnp.bfloat16)).astype(jnp.float32)
    blocks = lattice.reshape(3, row_count // NB, NB, narrow // NB, NB, 2, momenta)
    mixed_list = []
    for target in range(3):
        first_w = weights[2 * target][None, :, None, :, None, :]
        second_w = weights[2 * target + 1][None, :, None, :, None, :]
        summed = first_w * blocks[(target + 1) % 3] + second_w * blocks[(target + 2) % 3]
        mixed_list.append(summed.astype(jnp.bfloat16).reshape(row_count, narrow, 2, momenta))
    mixed_all = jnp.stack(mixed_list)
    projected = jnp.einsum(
        "tanpr,prsq->tqasn", mixed_all, backward, preferred_element_type=jnp.float32
    ).astype(jnp.bfloat16)
    returned_proj = lax.all_to_all(projected, "pb", split_axis=1, concat_axis=4, tiled=True)
    returned_proj = returned_proj.reshape(3, mesh_z, row_count, 2 * full_order)
    united_rows = (vertex.astype(jnp.float32) + returned_proj.astype(jnp.float32)).astype(
        jnp.bfloat16
    )
    united = lax.all_to_all(united_rows, "col", split_axis=1, concat_axis=2, tiled=True)
    local_q = united.shape[1]
    flat_united = united.reshape(3 * local_q, full_order, 2 * full_order)
    flat_loops = loop_blocks.reshape(3 * local_q, full_order, 2 * full_order)
    middle = complex_batch(flat_united, flat_loops).astype(jnp.bfloat16)
    change = complex_batch(middle, flat_united)
    increment = (
        (step_length * change).astype(jnp.bfloat16).reshape(3, local_q, full_order, 2 * full_order)
    )
    returned = lax.all_to_all(increment, "col", split_axis=2, concat_axis=1, tiled=True)
    return (vertex.astype(jnp.float32) + returned.astype(jnp.float32)).astype(jnp.bfloat16)


def solution(mesh):
    return jax.shard_map(
        per_device,
        mesh=mesh,
        in_specs=(P(None, "pb", "col", None), P(None, ("pb", "col"), None, None), P(), P()),
        out_specs=P(None, "pb", "col", None),
        check_vma=False,
    )
```

profile of v0, /device:TPU:32, one launch (start us, length us, event | category | flops | bytes accessed | tf_op | source)
XLA Modules:
  0.0 358.5 jit_solution(17212420372139971582)
XLA Ops:
  0.0 8.3 %reshape.772 = bf16[3,4,112,2,448]{4,3,2,1,0:T(2,128)(2,1)} reshape(bf16[3,4,112,896]{3,2,1,0:T(8,128)(2,1)} %param.4) | data formatting | bytes 4816896 | tf_op jit(solution)/shard_map/reshape | solution.py:74
  8.3 10.9 %copy.113 = bf16[3,4,112,2,448]{2,3,1,0,4:T(2,128)(2,1)} copy(bf16[3,4,112,2,448]{4,3,2,1,0:T(2,128)(2,1)} %reshape.772) | data formatting | bytes 4816896 | tf_op jit(solution)/shard_map/reshape | solution.py:74
  19.3 12.0 %all-to-all-start = ((bf16[3,4,112,2,448]{2,3,1,0,4:T(2,128)(2,1)}), bf16[3,4,112,2,448]{2,3,1,0,4:T(2,128)(2,1)}, u32[]{:S(2)}, u32[]{:S(2)}) async-start(bf16[3,4,112,2,448]{2,3,1,0,4:T(2,128)(2,1)} %copy.113), calls=%async_computation | async-start | bytes 5505024 | tf_op jit(solution)/shard_map/all_to_all | solution.py:75
  31.7 23.8 %gather_fusion = f32[12544,6]{1,0:T(8,128)} fusion(f32[6,256]{0,1:T(8,128)S(1)} %copy.109, s32[13312]{0:T(1024)S(1)} %pad_clamp_fusion), kind=kCustom, calls=%fused_computation | custom fusion | bytes 652288 | tf_op jit(solution)/shard_map/jit(_take)/gather | solution.py:44
  55.5 4.8 %copy.110 = f32[7,7,256,6]{2,1,0,3:T(8,128)S(1)} copy(f32[7,7,256,6]{3,2,1,0:T(8,128)} %bitcast.112) | data formatting | bytes 602112 | tf_op jit(solution)/shard_map/jit(_take)/gather | solution.py:44
  60.8 0.6 copy.118
  61.5 1.0 mul.482
  62.5 0.9 mul.486
  63.4 1.0 mul.487
  64.5 1.1 mul.492
  65.6 1.0 mul.497
  66.7 1.0 mul.502
  67.8 1.0 mul.475
  68.8 1.2 fusion.36
  70.0 0.9 maximum_bitcast_fusion.3
  70.9 25.4 %all-to-all-done = bf16[3,4,112,2,448]{2,3,1,0,4:T(2,128)(2,1)} async-done(((bf16[3,4,112,2,448]{2,3,1,0,4:T(2,128)(2,1)}), bf16[3,4,112,2,448]{2,3,1,0,4:T(2,128)(2,1)}, u32[]{:S(2)}, u32[]{:S(2)}) %all-to-all-start) | async-done | bytes 2408480 | tf_op jit(solution)/shard_map/all_to_all | solution.py:75
  96.3 3.0 copy.115
  99.4 1.5 fusion.8
  100.9 0.6 convert_element_type.113
  101.5 0.5 copy-done.2
  102.0 0.2 copy-done.3
  102.2 0.2 copy-done.4
  102.5 0.2 copy-done.5
  102.7 0.2 copy-done.6
  103.0 0.2 copy-done.7
  103.2 1.1 add_convert_fusion.2
  104.3 2.8 fusion.7
  107.2 8.6 %copy.124 = bf16[3,256,112,2,7]{2,3,4,0,1:T(2,128)(2,1)} copy(bf16[3,256,112,2,7]{1,2,4,0,3:T(8,128)(2,1)} %fusion.7) | data formatting | bytes 4816896 | tf_op jit(solution)/shard_map/convert_element_type | solution.py:90
  115.8 69.9 %all_to_all.45 = bf16[3,256,112,2,7]{2,3,4,0,1:T(2,128)(2,1)S(1)} all-to-all(bf16[3,256,112,2,7]{2,3,4,0,1:T(2,128)(2,1)} %copy.124), channel_id=1, replica_groups=mesh['pb'=64,'col'=4] {'pb'}, dimensions={1} | all-to-all | bytes 4816896 | tf_op jit(solution)/shard_map/all_to_all | solution.py:91
  185.7 0.6 copy.125
  186.4 0.7 convert_bitcast_fusion
  187.0 3.3 copy.126
  190.4 7.2 %copy.127 = f32[3,4,112,896]{3,2,1,0:T(8,128)} copy(f32[3,4,112,896]{2,1,3,0:T(4,128)} %bitcast.109) | data formatting | bytes 9633792 | tf_op jit(solution)/shard_map/convert_element_type | solution.py:93
  197.5 3.6 %fusion = bf16[3,4,112,896]{3,2,1,0:T(8,128)(2,1)S(1)} fusion(f32[3,4,112,896]{3,2,1,0:T(8,128)} %copy.127, bf16[3,4,112,896]{3,2,1,0:T(8,128)(2,1)} %param.4), kind=kLoop, calls=%fused_computation.4 | loop fusion | flops 3612672 | bytes 9633792 | tf_op jit(solution)/shard_map/convert_element_type | solution.py:93
  201.2 0.2 copy.128
  201.4 64.0 %all_to_all.46 = bf16[3,4,112,896]{3,2,0,1:T(8,128)(2,1)S(1)} all-to-all(bf16[3,4,112,896]{3,2,0,1:T(8,128)(2,1)S(1)} %copy.128), channel_id=1, replica_groups=mesh['pb'=64,'col'=4] {'col'}, dimensions={1} | all-to-all | bytes 4816896 | tf_op jit(solution)/shard_map/all_to_all | solution.py:96
  265.4 0.2 copy.129
  265.6 1.7 fusion.9
  267.2 1.6 fusion.11
  268.8 1.7 fusion.20
  270.5 1.7 fusion.18
  272.2 1.5 fusion.4
  273.7 0.9 fusion.2
  274.6 2.1 copy.130
  276.6 78.2 %all_to_all.47 = bf16[3,1,448,896]{3,0,1,2:T(4,128)(2,1)S(1)} all-to-all(bf16[3,1,448,896]{3,0,1,2:T(4,128)(2,1)S(1)} %copy.130), channel_id=1, replica_groups=mesh['pb'=64,'col'=4] {'col'}, dimensions={2} | all-to-all | bytes 4816896 | tf_op jit(solution)/shard_map/all_to_all | solution.py:105
  354.8 0.3 copy.131
  355.1 1.4 copy-done.1
  356.5 2.0 fusion.1
  (51 shorter events, 1.2 us)
Async XLA Ops:
  0.0 265.6 %copy-start = (bf16[3,1,448,896]{3,2,1,0:T(8,128)(2,1)S(1)}, bf16[3,1,448,896]{3,2,1,0:T(8,128)(2,1)}, u32[]{:S(2)}) copy-start(bf16[3,1,448,896]{3,2,1,0:T(8,128)(2,1)} %param.5) | copy-start | bytes 7225348
  19.3 12.0 %copy-start.17 = (s32[7,3]{0,1:T(4,128)S(1)}, s32[7,3]{0,1:T(4,128)}, u32[]{:S(2)}) copy-start(s32[7,3]{0,1:T(4,128)} %param.7) | copy-start | bytes 256
  19.3 12.3 %copy-start.16 = (f32[6,256]{1,0:T(8,128)S(1)}, f32[6,256]{1,0:T(8,128)}, u32[]{:S(2)}) copy-start(f32[6,256]{1,0:T(8,128)} %param.6) | copy-start | bytes 18436
  19.3 77.0 %all-to-all-start = ((bf16[3,4,112,2,448]{2,3,1,0,4:T(2,128)(2,1)}), bf16[3,4,112,2,448]{2,3,1,0,4:T(2,128)(2,1)}, u32[]{:S(2)}, u32[]{:S(2)}) async-start(bf16[3,4,112,2,448]{2,3,1,0,4:T(2,128)(2,1)} %copy.113), calls=%async_computation | async-start | bytes 5505024 | tf_op jit(solution)/shard_map/all_to_all | solution.py:75
  31.3 29.1 %copy-start.14 = (s32[256]{0:T(256)}, s32[256]{0:T(256)S(1)}, u32[]{:S(2)}) copy-start(s32[256]{0:T(256)S(1)} %and_select_fusion.3) | copy-start | bytes 3076
  31.3 29.1 %copy-start.10 = (s32[256]{0:T(256)}, s32[256]{0:T(256)S(1)}, u32[]{:S(2)}) copy-start(s32[256]{0:T(256)S(1)} %get-tuple-element.29) | copy-start | bytes 3076
  31.3 29.1 %copy-start.12 = (s32[256]{0:T(256)}, s32[256]{0:T(256)S(1)}, u32[]{:S(2)}) copy-start(s32[256]{0:T(256)S(1)} %get-tuple-element.30) | copy-start | bytes 3076
  66.6 2.2 copy-start.11
  66.6 2.2 copy-start.13
  66.6 2.2 copy-start.15
  100.8 1.1 copy-start.2
  100.8 1.4 copy-start.3
  100.9 1.6 copy-start.4
  100.9 1.8 copy-start.5
  100.9 2.1 copy-start.6
  100.9 2.3 copy-start.7
  103.2 1.1 copy-start.8
  103.2 1.1 copy-start.9
  354.8 1.7 copy-start.1
where the time goes:
time: 360 us; the launch traced here: 359 us
  blocking collectives  212 us (59%)
  local copies, waits for them, and re-layouts  84.8 us (24%)
  waiting for transfers between devices  25.4 us (7%)
  other arithmetic  13 us (4%)
  starting transfers between devices  12 us (3%)
  matrix products  10.9 us (3%)
    all_to_all x1, blocking collectives, per_device(): lax.all_to_all(increment, 'col', split_axis=2, concat_axis=1, tiled=True)  78.2 us
    all_to_all x1, blocking collectives, per_device(): lax.all_to_all(projected, 'pb', split_axis=1, concat_axis=4, tiled=True)  69.9 us
    all_to_all x1, blocking collectives, per_device(): lax.all_to_all(united_rows, 'col', split_axis=1, concat_axis=2, tiled=True)  64 us
    gather x2, local copies, waits for them, and re-layouts, shifted_weights(): return jnp.take(mixing, flat_slot, axis=1)  28.6 us
    all_to_all x1, waiting for transfers between devices, per_device(): lax.all_to_all(split_cols, 'pb', split_axis=4, concat_axis=1, tiled=True)  25.4 us
    reshape x2, local copies, waits for them, and re-layouts, per_device(): split_cols = vertex.reshape(3, mesh_z, row_count, 2, full_order)  19.3 us
    all_to_all x1, starting transfers between devices, per_device(): lax.all_to_all(split_cols, 'pb', split_axis=4, concat_axis=1, tiled=True)  12 us
    convert_element_type x2, local copies, waits for them, and re-layouts, per_device(): returned_proj.astype(jnp.float32)  10.5 us
  transfers between devices with their start and end apart: 1, of which 1 were waited for; matrix products, arithmetic and copies ran while one was open for 11% of the time, Pallas kernels for 0%

commit v1 on v0

--- a/solution.py
+++ b/solution.py
@@ -93,7 +93,9 @@
     united_rows = (vertex.astype(jnp.float32) + returned_proj.astype(jnp.float32)).astype(
         jnp.bfloat16
     )
-    united = lax.all_to_all(united_rows, "col", split_axis=1, concat_axis=2, tiled=True)
+    shards = jnp.split(united_rows, lax.axis_size("col"), axis=1)
+    got = lax.all_to_all(jnp.stack(shards), "col", 0, 0)
+    united = jnp.concatenate(got, axis=2)
     local_q = united.shape[1]
     flat_united = united.reshape(3 * local_q, full_order, 2 * full_order)
     flat_loops = loop_blocks.reshape(3 * local_q, full_order, 2 * full_order)

time: 360 us -> 390 us (1.083)
  the two profiles are of different devices: /device:TPU:32 before, /device:TPU:38 now
where the time goes in v1:
time: 390 us; the launch traced here: 389 us
  blocking collectives  143 us (37%)
  local copies, waits for them, and re-layouts  118 us (30%)
  waiting for transfers between devices  79.7 us (20%)
  starting transfers between devices  20.1 us (5%)
  other arithmetic  16.9 us (4%)
  matrix products  10.9 us (3%)
    all_to_all x1, blocking collectives, per_device(): lax.all_to_all(increment, 'col', split_axis=2, concat_axis=1, tiled=True)  78.4 us
    all_to_all x1, blocking collectives, per_device(): got = lax.all_to_all(jnp.stack(shards), 'col', 0, 0)  64.2 us
    all_to_all x1, waiting for transfers between devices, per_device(): lax.all_to_all(projected, 'pb', split_axis=1, concat_axis=4, tiled=True)  56.3 us
    gather x2, local copies, waits for them, and re-layouts, shifted_weights(): return jnp.take(mixing, flat_slot, axis=1)  28.8 us
    all_to_all x1, waiting for transfers between devices, per_device(): lax.all_to_all(split_cols, 'pb', split_axis=4, concat_axis=1, tiled=True)  23.4 us
    split x5, local copies, waits for them, and re-layouts, per_device(): shards = jnp.split(united_rows, lax.axis_size('col'), axis=1)  22.7 us
    reshape x2, local copies, waits for them, and re-layouts, per_device(): split_cols = vertex.reshape(3, mesh_z, row_count, 2, full_order)  19.3 us
    all_to_all x1, starting transfers between devices, per_device(): lax.all_to_all(split_cols, 'pb', split_axis=4, concat_axis=1, tiled=True)  12.1 us
  transfers between devices with their start and end apart: 2, of which 2 were waited for; matrix products, arithmetic and copies ran while one was open for 12% of the time, Pallas kernels for 0%

profile of v1, /device:TPU:38, one launch (start us, length us, event | category | flops | bytes accessed | tf_op | source)
XLA Modules:
  0.0 388.5 jit_solution(7275121328408365513)
XLA Ops:
  0.0 8.3 %reshape.768 = bf16[3,4,112,2,448]{4,3,2,1,0:T(2,128)(2,1)} reshape(bf16[3,4,112,896]{3,2,1,0:T(8,128)(2,1)} %param.4) | data formatting | bytes 4816896 | tf_op jit(solution)/shard_map/reshape | solution.py:74
  8.3 11.0 %copy.201 = bf16[3,4,112,2,448]{2,3,1,0,4:T(2,128)(2,1)} copy(bf16[3,4,112,2,448]{4,3,2,1,0:T(2,128)(2,1)} %reshape.768) | data formatting | bytes 4816896 | tf_op jit(solution)/shard_map/reshape | solution.py:74
  19.3 12.1 %all-to-all-start = ((bf16[3,4,112,2,448]{2,3,1,0,4:T(2,128)(2,1)}), bf16[3,4,112,2,448]{2,3,1,0,4:T(2,128)(2,1)}, u32[]{:S(2)}, u32[]{:S(2)}) async-start(bf16[3,4,112,2,448]{2,3,1,0,4:T(2,128)(2,1)} %copy.201), calls=%async_computation | async-start | bytes 5505024 | tf_op jit(solution)/shard_map/all_to_all | solution.py:75
  31.9 23.9 %gather_fusion = f32[12544,6]{1,0:T(8,128)} fusion(f32[6,256]{0,1:T(8,128)S(1)} %copy.197, s32[13312]{0:T(1024)S(1)} %pad_clamp_fusion), kind=kCustom, calls=%fused_computation | custom fusion | bytes 652288 | tf_op jit(solution)/shard_map/jit(_take)/gather | solution.py:44
  55.8 4.8 %copy.198 = f32[7,7,256,6]{2,1,0,3:T(8,128)S(1)} copy(f32[7,7,256,6]{3,2,1,0:T(8,128)} %bitcast.118) | data formatting | bytes 602112 | tf_op jit(solution)/shard_map/jit(_take)/gather | solution.py:44
  61.1 0.6 copy.206
  61.8 1.0 mul.482
  62.8 0.9 mul.486
  63.7 1.0 mul.487
  64.8 1.1 mul.492
  65.9 1.0 mul.497
  67.0 1.0 mul.502
  68.1 1.0 mul.475
  69.1 1.2 fusion.36
  70.3 0.8 maximum_bitcast_fusion.3
  71.3 23.4 %all-to-all-done = bf16[3,4,112,2,448]{2,3,1,0,4:T(2,128)(2,1)} async-done(((bf16[3,4,112,2,448]{2,3,1,0,4:T(2,128)(2,1)}), bf16[3,4,112,2,448]{2,3,1,0,4:T(2,128)(2,1)}, u32[]{:S(2)}, u32[]{:S(2)}) %all-to-all-start) | async-done | bytes 2408480 | tf_op jit(solution)/shard_map/all_to_all | solution.py:75
  94.7 3.0 copy.203
  97.7 1.5 fusion.8
  101.5 1.1 add_convert_fusion.2
  102.7 2.8 fusion.7
  105.5 8.6 %copy.212 = bf16[3,256,112,2,7]{2,3,4,0,1:T(2,128)(2,1)} copy(bf16[3,256,112,2,7]{1,2,4,0,3:T(8,128)(2,1)} %fusion.7) | data formatting | bytes 4816896 | tf_op jit(solution)/shard_map/convert_element_type | solution.py:90
  114.1 8.0 %all-to-all-start.1 = ((bf16[3,256,112,2,7]{2,3,4,0,1:T(2,128)(2,1)}), bf16[3,256,112,2,7]{2,3,4,0,1:T(2,128)(2,1)}, u32[]{:S(2)}, u32[]{:S(2)}) async-start(bf16[3,256,112,2,7]{2,3,4,0,1:T(2,128)(2,1)} %copy.212), calls=%async_computation.1 | async-start | bytes 5505024 | tf_op jit(solution)/shard_map/all_to_all | solution.py:91
  122.1 5.7 %copy.196 = bf16[3,4,112,896]{2,1,3,0:T(4,128)(2,1)} copy(bf16[3,4,112,896]{3,2,1,0:T(8,128)(2,1)} %param.4) | data formatting | bytes 4816896 | tf_op args[0]
  127.8 56.3 %all-to-all-done.1 = bf16[3,256,112,2,7]{2,3,4,0,1:T(2,128)(2,1)} async-done(((bf16[3,256,112,2,7]{2,3,4,0,1:T(2,128)(2,1)}), bf16[3,256,112,2,7]{2,3,4,0,1:T(2,128)(2,1)}, u32[]{:S(2)}, u32[]{:S(2)}) %all-to-all-start.1) | async-done | bytes 2408480 | tf_op jit(solution)/shard_map/all_to_all | solution.py:91
  184.2 2.4 copy.213
  186.6 0.7 convert_bitcast_fusion
  187.3 0.9 copy.214
  188.2 0.8 copy-done.1
  189.0 1.4 fusion
  190.5 5.5 %fusion.57 = (bf16[3,1,112,896]{2,1,3,0:T(2,128)(2,1)}, bf16[3,1,112,896]{2,1,3,0:T(2,128)(2,1)}, bf16[3,1,112,896]{2,1,3,0:T(2,128)(2,1)}, bf16[3,1,112,896]{2,1,3,0:T(2,128)(2,1)}) fusion(bf16[3,4,112,896]{2,1,3,0:T(4,128)(2,1)S(1)} %fusion), kind=kLoop, calls=%fused_computation.133 | loop fusion | bytes 4816896 | tf_op jit(solution)/shard_map/split | solution.py:96
  195.9 3.5 copy.215
  199.4 4.6 %copy.218 = bf16[3,1,112,896]{3,2,0,1:T(8,128)(2,1)} copy(bf16[3,1,112,896]{2,1,3,0:T(2,128)(2,1)} %get-tuple-element.11) | data formatting | bytes 1204224 | tf_op jit(solution)/shard_map/split | solution.py:96
  204.0 4.6 %copy.217 = bf16[3,1,112,896]{3,2,0,1:T(8,128)(2,1)} copy(bf16[3,1,112,896]{2,1,3,0:T(2,128)(2,1)} %get-tuple-element.12) | data formatting | bytes 1204224 | tf_op jit(solution)/shard_map/split | solution.py:96
  208.6 4.6 %copy.216 = bf16[3,1,112,896]{3,2,0,1:T(8,128)(2,1)} copy(bf16[3,1,112,896]{2,1,3,0:T(2,128)(2,1)} %get-tuple-element.13) | data formatting | bytes 1204224 | tf_op jit(solution)/shard_map/split | solution.py:96
  213.1 1.8 pad_maximum_fusion.1
  214.9 64.2 %all_to_all.41 = bf16[4,3,1,112,896]{4,3,1,2,0:T(8,128)(2,1)S(1)} all-to-all(bf16[4,3,1,112,896]{4,3,1,2,0:T(8,128)(2,1)S(1)} %pad_maximum_fusion.1), channel_id=1, replica_groups=mesh['pb'=64,'col'=4] {'col'}, dimensions={0} | all-to-all | bytes 4816896 | tf_op jit(solution)/shard_map/all_to_all | solution.py:97
  279.3 1.7 fusion.9
  281.0 1.6 fusion.11
  282.6 1.7 fusion.20
  284.2 1.7 fusion.18
  285.9 1.5 fusion.4
  287.4 0.9 fusion.2
  288.3 2.1 copy.220
  290.4 78.4 %all_to_all.42 = bf16[3,1,448,896]{3,0,1,2:T(4,128)(2,1)S(1)} all-to-all(bf16[3,1,448,896]{3,0,1,2:T(4,128)(2,1)S(1)} %copy.220), channel_id=1, replica_groups=mesh['pb'=64,'col'=4] {'col'}, dimensions={2} | all-to-all | bytes 4816896 | tf_op jit(solution)/shard_map/all_to_all | solution.py:107
  368.7 1.7 copy.221
  370.5 6.0 %copy.222 = f32[3,4,112,896]{2,1,3,0:T(4,128)} copy(bf16[3,4,112,896]{3,2,1,0:T(8,128)(2,1)} %bitcast.117) | data formatting | bytes 7225344 | tf_op jit(solution)/shard_map/convert_element_type | solution.py:108
  376.4 6.4 %fusion.1 = bf16[3,4,112,896]{2,1,3,0:T(4,128)(2,1)} fusion(f32[3,4,112,896]{2,1,3,0:T(4,128)} %copy.222, bf16[3,4,112,896]{2,1,3,0:T(4,128)(2,1)} %copy.196), kind=kLoop, calls=%fused_computation.4 | loop fusion | flops 3612672 | bytes 9633792 | tf_op jit(solution)/shard_map/convert_element_type | solution.py:108
  382.8 5.7 %copy.223 = bf16[3,4,112,896]{3,2,1,0:T(8,128)(2,1)} copy(bf16[3,4,112,896]{2,1,3,0:T(4,128)(2,1)} %fusion.1) | data formatting | bytes 4816896 | tf_op jit(solution)/shard_map/convert_element_type | solution.py:108
  (59 shorter events, 3.7 us)
Async XLA Ops:
  0.0 279.3 %copy-start = (bf16[3,1,448,896]{3,2,1,0:T(8,128)(2,1)S(1)}, bf16[3,1,448,896]{3,2,1,0:T(8,128)(2,1)}, u32[]{:S(2)}) copy-start(bf16[3,1,448,896]{3,2,1,0:T(8,128)(2,1)} %param.5) | copy-start | bytes 7225348
  19.3 12.1 %copy-start.17 = (s32[7,3]{0,1:T(4,128)S(1)}, s32[7,3]{0,1:T(4,128)}, u32[]{:S(2)}) copy-start(s32[7,3]{0,1:T(4,128)} %param.7) | copy-start | bytes 256
  19.3 12.4 %copy-start.16 = (f32[6,256]{1,0:T(8,128)S(1)}, f32[6,256]{1,0:T(8,128)}, u32[]{:S(2)}) copy-start(f32[6,256]{1,0:T(8,128)} %param.6) | copy-start | bytes 18436
  19.3 75.3 %all-to-all-start = ((bf16[3,4,112,2,448]{2,3,1,0,4:T(2,128)(2,1)}), bf16[3,4,112,2,448]{2,3,1,0,4:T(2,128)(2,1)}, u32[]{:S(2)}, u32[]{:S(2)}) async-start(bf16[3,4,112,2,448]{2,3,1,0,4:T(2,128)(2,1)} %copy.201), calls=%async_computation | async-start | bytes 5505024 | tf_op jit(solution)/shard_map/all_to_all | solution.py:75
  31.4 29.3 %copy-start.14 = (s32[256]{0:T(256)}, s32[256]{0:T(256)S(1)}, u32[]{:S(2)}) copy-start(s32[256]{0:T(256)S(1)} %and_select_fusion.3) | copy-start | bytes 3076
  31.5 29.2 %copy-start.10 = (s32[256]{0:T(256)}, s32[256]{0:T(256)S(1)}, u32[]{:S(2)}) copy-start(s32[256]{0:T(256)S(1)} %get-tuple-element.33) | copy-start | bytes 3076
  31.5 29.2 %copy-start.12 = (s32[256]{0:T(256)}, s32[256]{0:T(256)S(1)}, u32[]{:S(2)}) copy-start(s32[256]{0:T(256)S(1)} %get-tuple-element.34) | copy-start | bytes 3076
  67.0 2.1 copy-start.11
  67.0 2.1 copy-start.13
  67.0 2.1 copy-start.15
  99.2 1.1 copy-start.2
  99.2 1.4 copy-start.3
  99.2 1.6 copy-start.4
  99.2 1.8 copy-start.5
  99.2 2.1 copy-start.6
  99.2 2.3 copy-start.7
  101.5 1.1 copy-start.8
  101.5 1.1 copy-start.9
  114.1 70.0 %all-to-all-start.1 = ((bf16[3,256,112,2,7]{2,3,4,0,1:T(2,128)(2,1)}), bf16[3,256,112,2,7]{2,3,4,0,1:T(2,128)(2,1)}, u32[]{:S(2)}, u32[]{:S(2)}) async-start(bf16[3,256,112,2,7]{2,3,4,0,1:T(2,128)(2,1)} %copy.212), calls=%async_computation.1 | async-start | bytes 5505024 | tf_op jit(solution)/shard_map/all_to_all | solution.py:91
  187.3 1.8 copy-start.1
